TPU v7x, 256 devices: a whole 4x4x8 slice. The times are simulated.
256 devices in a mesh: pair: 16 (over z, core), red: 16 (over x, y).
Axes of the slice: x: 4, y: 4, z: 8, core: 2. Of those that a mesh axis runs over, the one named last changes fastest.
Arguments:
- three_center: bfloat16 [2304, 256, 256], P('pair', 'red'), may hold values from -0.375 to 0.375
- occ_src: int32 [256, 16], P('red'), may hold values from 0 to 15, as said below
- occ_block: int32 [256, 16], P('red'), may hold values from 0 to 31
- occ_blocks: bfloat16 [512, 256], P('red'), may hold values from -0.375 to 0.375
- virt_block: int32 [16, 16, 1], P('red'), may hold values from 0 to 31, as said below
- virt_blocks: bfloat16 [16, 32, 256], P('red', 'pair'), may hold values from -1.5 to 1.5
Outputs:
- chi: float32 [2304, 2304], P('pair', 'red')
Inputs may be any that keep to these rules, and one draw needn't show every extreme that they name: `occ_src`: the 16 entries of a row are distinct. `virt_block`: every block listed for tile t of a red group lies from (t) * 2 to (t) * 2 + 1.
All inputs are finite; a program needn't handle non-finite values.
Results may differ from a plain program's by a relative error of at most 0.0041.
Values may be sent and summed in bfloat16 or wider, within the bound.
A program may use at most 128 MiB of HBM per device.

v0:
```python
import jax
import jax.numpy as jnp
from jax import lax
from jax.sharding import PartitionSpec as P

BLK = 16
TPD = 1


def occupied(three_center, occ_src, occ_block, occ_blocks):
    aux_rows, ntiles, area = three_center.shape
    nblocks = occ_blocks.shape[0]
    block_hot = (
        occ_block[:, :, None] == jnp.arange(nblocks, dtype=jnp.int32)[None, None, :]
    ).astype(jnp.bfloat16)
    picked = jnp.einsum(
        "tsb,bk->tsk", block_hot, occ_blocks, preferred_element_type=jnp.float32
    ).astype(jnp.bfloat16)
    source_hot = (occ_src[:, :, None] == jnp.arange(ntiles, dtype=jnp.int32)[None, None, :]).astype(
        jnp.bfloat16
    )
    mixing = jnp.einsum(
        "tsk,tsa->tka", source_hot, picked, preferred_element_type=jnp.float32
    ).astype(jnp.bfloat16)
    mixing = mixing.reshape(ntiles, ntiles, BLK, BLK)
    blocks = three_center.reshape(aux_rows, ntiles, BLK, BLK)
    half = jnp.einsum("tkml,pkln->ptmn", mixing, blocks, preferred_element_type=jnp.float32)
    return half.reshape(aux_rows, ntiles, area).astype(jnp.bfloat16)


def virtual(half, listed, blocks):
    aux_rows, ntiles, area = half.shape
    owners = listed.shape[0]
    nblocks = blocks.shape[0]
    block_hot = (listed[..., None] == jnp.arange(nblocks, dtype=jnp.int32)).astype(jnp.bfloat16)
    picked = jnp.einsum(
        "oijb,bk->oijk", block_hot, blocks, preferred_element_type=jnp.float32
    ).astype(jnp.bfloat16)
    picked = picked.reshape(owners, TPD, TPD, BLK, BLK)
    grouped = half.reshape(aux_rows, owners, TPD, BLK, BLK)
    kernel = jnp.einsum("pojml,oijln->poimn", grouped, picked, preferred_element_type=jnp.float32)
    return kernel.reshape(aux_rows, ntiles, area).astype(jnp.bfloat16)


def shards(three_center, occ_src, occ_block, occ_blocks, virt_block, virt_blocks):
    aux_rows, ntiles, area = three_center.shape
    half = occupied(three_center, occ_src, occ_block, occ_blocks)
    own_blocks = virt_blocks[0]
    listed = virt_block[0]
    all_blocks = lax.all_gather(own_blocks, "pair", axis=0, tiled=True)
    kernel = virtual(half, listed.reshape(ntiles // TPD, TPD, TPD), all_blocks)
    flat_tiles = three_center.reshape(aux_rows, ntiles * area)
    piece = lax.all_gather(kernel, "pair", axis=0, tiled=True)
    flat_piece = piece.reshape(piece.shape[0], ntiles * area)
    partial_value = lax.dot_general(
        flat_tiles, flat_piece, (((1,), (1,)), ((), ())), preferred_element_type=jnp.float32
    )
    return lax.psum_scatter(partial_value, "red", scatter_dimension=1, tiled=True)


def solution(mesh):
    placed = (
        P("pair", "red", None),
        P("red", None),
        P("red", None),
        P("red", None),
        P("red", None, None),
        P("red", "pair", None),
    )
    return jax.shard_map(
        shards, mesh=mesh, in_specs=placed, out_specs=P("pair", "red"), check_vma=False
    )
```

profile of v0, /device:TPU:32, one launch (start us, length us, event | category | flops | bytes accessed | tf_op | source)
XLA Modules:
  0.0 243.4 jit_solution(1345893647742258906)
XLA Ops:
  6.5 0.0 copy-start
  6.5 0.0 copy-start.1
  6.5 0.0 all-gather.3.cloned.1.call-start
  6.5 0.8 copy.21
  7.3 17.9 %all-gather = bf16[1,32,256]{2,0,1:T(2,128)(2,1)S(1)} all-gather(bf16[1,2,256]{2,0,1:T(2,128)(2,1)S(1)} %copy.21), channel_id=2, replica_groups=mesh['pair'=16,'red'=16] {'pair'}, dimensions={1}, use_global_device_ids=true | all-gather | bytes 17408 | tf_op jit(solution)/shard_map/all_gather | solution.py:50
  25.2 0.8 convolution_convert_fusion.2
  26.1 0.1 reshape.42
  26.2 0.0 copy-done
  26.2 1.1 convolution_convert_fusion
  27.3 1.7 reshape.47
  29.0 0.0 copy-done.1
  29.0 1.2 copy.22
  30.2 3.4 %fusion.7 = bf16[144,16,16,16]{0,2,3,1:T(8,128)(2,1)S(1)} fusion(bf16[144,16,16,16]{0,3,2,1:T(8,128)(2,1)S(1)} %bitcast.43, bf16[16,16,16,16,1]{3,2,1,0,4:T(8,128)(2,1)} %reshape.47), kind=kOutput, calls=%fused_computation.7 | convolution fusion | flops 302579712 | bytes 2490368 | tf_op jit(solution)/shard_map/tkml,pkln->ptmn/dot_general | solution.py:27
  33.5 2.2 fusion.4
  35.7 3.7 %copy.26 = bf16[144,16,256]{2,0,1:T(8,128)(2,1)} copy(bf16[144,16,256]{0,2,1:T(8,128)(2,1)} %bitcast.44) | data formatting | bytes 2359296 | tf_op jit(solution)/shard_map/convert_element_type | solution.py:42
  39.4 0.0 all-gather.3.cloned.1.call-update
  39.4 0.0 reduce-scatter.4.cloned.1.call-start
  39.5 103.4 %all-gather.3.cloned.1.call-done = bf16[2304,16,256]{2,0,1:T(8,128)(2,1)} async-done(((bf16[144,16,256]{2,0,1:T(8,128)(2,1)}), bf16[2304,16,256]{2,0,1:T(8,128)(2,1)}) %all-gather.3.cloned.1.call-update) | async-done | bytes 18874384 | tf_op jit(solution)/shard_map/all_gather | solution.py:53
  142.8 9.5 %convolution_bitcast_fusion = f32[144,2304]{1,0:T(8,128)S(1)} fusion(bf16[2304,16,256]{2,0,1:T(8,128)(2,1)} %all-gather.3.cloned.1.call-done, bf16[144,16,256]{0,2,1:T(8,128)(2,1)S(1)} %copy.22), kind=kOutput, calls=%fused_computation.1 | convolution fusion | flops 2717908992 | bytes 21381120 | tf_op jit(solution)/shard_map/dot_general | solution.py:55
  152.3 1.9 copy.33
  154.2 0.0 reduce-scatter.4.cloned.1.call-update
  154.3 80.6 %reduce-scatter.4.cloned.1.call-done = f32[144,144]{1,0:T(8,128)} async-done(((f32[2304,144]{1,0:T(8,128)}), f32[144,144]{1,0:T(8,128)}) %reduce-scatter.4.cloned.1.call-update) | async-done | bytes 82960
  234.9 1.7 copy.34
Async XLA Ops:
  6.5 19.6 %copy-start = (bf16[32,256]{1,0:T(8,128)(2,1)S(1)}, bf16[32,256]{1,0:T(8,128)(2,1)}, u32[]{:S(2)}) copy-start(bf16[32,256]{1,0:T(8,128)(2,1)} %param.9) | copy-start | bytes 49156
  6.5 22.4 %copy-start.1 = (bf16[144,16,256]{2,1,0:T(8,128)(2,1)S(1)}, bf16[144,16,256]{2,1,0:T(8,128)(2,1)}, u32[]{:S(2)}) copy-start(bf16[144,16,256]{2,1,0:T(8,128)(2,1)} %param.6) | copy-start | bytes 3538948
  6.5 136.3 %all-gather.3.cloned.1.call-start = ((), (), s32[]{:S(2)}) async-start(), calls=%async_computation.1 | async-start | bytes 20054016 | tf_op jit(solution)/shard_map/all_gather | solution.py:53
  39.4 195.4 %reduce-scatter.4.cloned.1.call-start = ((), (), s32[]{:S(2)}) async-start(), calls=%async_computation.2 | async-start | bytes 2506752
Sparse Core Ops, SparseCore 0:
  39.6 103.2 all-gather.2
  154.4 80.4 reduce-scatter.3
where the time goes:
time: 244 us; the launch traced here: 243 us
  waiting for transfers between devices  184 us (75%)
  blocking collectives  17.9 us (7%)
  matrix products  17 us (7%)
  between operations  13.4 us (5%)
  local copies, waits for them, and re-layouts  11 us (5%)
    all_gather x1, waiting for transfers between devices, shards(): piece = lax.all_gather(kernel, 'pair', axis=0, tiled=True)  103 us
    unnamed x3, waiting for transfers between devices  80.6 us
    all_gather x1, blocking collectives, shards(): all_blocks = lax.all_gather(own_blocks, 'pair', axis=0, tiled=True)  17.9 us
    dot_general x1, matrix products, shards(): lax.dot_general(flat_tiles, flat_piece, (((1,), (1,)), ((), ())), preferr...  9.48 us
    unnamed x8, local copies, waits for them, and re-layouts  5.55 us
  transfers between devices with their start and end apart: 2, of which 2 were waited for; matrix products, arithmetic and copies ran while one was open for 0% of the time, Pallas kernels for 0%

commit v1 on v0

--- a/solution.py
+++ b/solution.py
@@ -47,7 +47,30 @@
     half = occupied(three_center, occ_src, occ_block, occ_blocks)
     own_blocks = virt_blocks[0]
     listed = virt_block[0]
-    all_blocks = lax.all_gather(own_blocks, "pair", axis=0, tiled=True)
+    current_value = lax.axis_size("pair")
+    r_now, arr_now, upper = (current_value, lax.axis_index("pair"), own_blocks.shape[0])
+    items = []
+    for it, s in enumerate(own_blocks.shape):
+        items.append(s * r_now if it == 0 else s)
+    plain = jnp.zeros(items, own_blocks.dtype)
+    all_blocks = lax.dynamic_update_slice_in_dim(plain, own_blocks, arr_now * upper, axis=0)
+    tall = part_next = own_blocks
+    for b in tuple(range(1, r_now // 2 + 1)):
+        rows = []
+        for it in [*range(r_now)]:
+            rows.append((it, (it + 1) % r_now))
+        tall = lax.ppermute(tall, "pair", rows)
+        all_blocks = lax.dynamic_update_slice_in_dim(
+            all_blocks, tall, (arr_now - b) % r_now * upper, axis=0
+        )
+        if 2 * b < r_now:
+            cards = []
+            for it in [*range(r_now)]:
+                cards.append((it, (it - 1) % r_now))
+            part_next = lax.ppermute(part_next, "pair", cards)
+            all_blocks = lax.dynamic_update_slice_in_dim(
+                all_blocks, part_next, (arr_now + b) % r_now * upper, axis=0
+            )
     kernel = virtual(half, listed.reshape(ntiles // TPD, TPD, TPD), all_blocks)
     flat_tiles = three_center.reshape(aux_rows, ntiles * area)
     piece = lax.all_gather(kernel, "pair", axis=0, tiled=True)

time: 244 us -> 262 us (1.074)
  waiting for transfers between devices: 184 us -> 202 us
  blocking collectives: 17.9 us -> 0 us
  starting transfers between devices: 0.04 us -> 16.8 us
    all_gather x1 -> x0, blocking collectives: 17.9 us -> none  [shards(): all_blocks = lax.all_gather(own_blocks, 'pair', axis=0, tiled=True)]
    ppermute x0 -> x15, starting transfers between devices: none -> 16.7 us  [the longest x7 16.4 us: shards(): part_next = lax.ppermute(part_next, 'pair', cards)]
    ppermute x0 -> x15, waiting for transfers between devices: none -> 11.6 us  [the longest x8 10.3 us: shards(): tall = lax.ppermute(tall, 'pair', rows)]
    all_gather x1, waiting for transfers between devices: 103 us -> 110 us  [shards(): piece = lax.all_gather(kernel, 'pair', axis=0, tiled=True)]
    unnamed x8 -> x11, local copies, waits for them, and re-layouts: 5.55 us -> 4.82 us
  transfers between devices with their start and end apart: 2 -> 17, of which waited for: 2 -> 15; matrix products, arithmetic and copies ran while one was open for 0% -> 3% of each run, Pallas kernels for 0% -> 0%
where the time goes in v1:
time: 262 us
  waiting for transfers between devices  202 us (77%)
  matrix products  18.9 us (7%)
  starting transfers between devices  16.8 us (6%)
  between operations  13.5 us (5%)
  local copies, waits for them, and re-layouts  10.4 us (4%)
    all_gather x1, waiting for transfers between devices, shards(): piece = lax.all_gather(kernel, 'pair', axis=0, tiled=True)  110 us
    unnamed x3, waiting for transfers between devices  80.7 us
    ppermute x7, starting transfers between devices, shards(): part_next = lax.ppermute(part_next, 'pair', cards)  16.4 us
    ppermute x8, waiting for transfers between devices, shards(): tall = lax.ppermute(tall, 'pair', rows)  10.3 us
    dot_general x1, matrix products, shards(): lax.dot_general(flat_tiles, flat_piece, (((1,), (1,)), ((), ())), preferr...  9.48 us
  transfers between devices with their start and end apart: 17, of which 15 were waited for; matrix products, arithmetic and copies ran while one was open for 3% of the time, Pallas kernels for 0%

profile of v1, /device:TPU:32, one launch (start us, length us, event | category | flops | bytes accessed | tf_op | source)
XLA Modules:
  0.0 261.8 jit_solution(7450951956108083363)
XLA Ops:
  6.5 0.0 collective-permute-start
  6.6 1.7 collective-permute-start.1
  8.3 1.1 convolution_convert_fusion
  9.4 0.0 copy-start.2
  9.4 1.7 reshape.46
  11.1 1.2 copy.14
  12.3 0.0 copy-start.3
  12.3 4.4 %fusion.7 = bf16[144,16,16,16]{0,2,3,1:T(8,128)(2,1)} fusion(bf16[144,16,16,16]{0,3,2,1:T(8,128)(2,1)S(1)} %bitcast.43, bf16[16,16,16,16,1]{3,2,1,0,4:T(8,128)(2,1)} %reshape.46), kind=kOutput, calls=%fused_computation.7 | convolution fusion | flops 302579712 | bytes 2490368 | tf_op jit(solution)/shard_map/tkml,pkln->ptmn/dot_general | solution.py:27
  16.7 0.0 collective-permute-done
  16.7 0.3 collective-permute-start.2
  17.0 0.0 collective-permute-done.1
  17.0 1.5 collective-permute-start.3
  18.5 1.2 collective-permute-done.2
  19.7 0.0 collective-permute-start.4
  19.7 0.1 collective-permute-done.3
  19.8 1.7 collective-permute-start.5
  21.5 1.2 collective-permute-done.4
  22.7 0.0 collective-permute-start.6
  22.7 0.1 collective-permute-done.5
  22.8 2.8 %collective-permute-start.7 = (bf16[2,256]{1,0:T(2,128)(2,1)S(1)}, bf16[2,256]{1,0:T(2,128)(2,1)S(1)}, u32[]{:S(2)}, u32[]{:S(2)}) collective-permute-start(bf16[2,256]{1,0:T(2,128)(2,1)S(1)} %collective-permute-done.5), channel_id=1, source_target_pairs={{0,240},{16,0},{32,16},{48,32},{64,48},{80,64},{96,80},{112,96},{1... | collective-permute-start | bytes 3080 | tf_op jit(solution)/shard_map/ppermute | solution.py:70
  25.6 1.0 collective-permute-done.6
  26.6 0.0 collective-permute-start.8
  26.6 0.3 collective-permute-done.7
  26.9 2.9 %collective-permute-start.9 = (bf16[2,256]{1,0:T(2,128)(2,1)S(1)}, bf16[2,256]{1,0:T(2,128)(2,1)S(1)}, u32[]{:S(2)}, u32[]{:S(2)}) collective-permute-start(bf16[2,256]{1,0:T(2,128)(2,1)S(1)} %collective-permute-done.7), channel_id=1, source_target_pairs={{0,240},{16,0},{32,16},{48,32},{64,48},{80,64},{96,80},{112,96},{1... | collective-permute-start | bytes 3080 | tf_op jit(solution)/shard_map/ppermute | solution.py:70
  29.8 1.0 collective-permute-done.8
  30.8 0.0 collective-permute-start.10
  30.8 0.3 collective-permute-done.9
  31.1 2.9 %collective-permute-start.11 = (bf16[2,256]{1,0:T(2,128)(2,1)S(1)}, bf16[2,256]{1,0:T(2,128)(2,1)S(1)}, u32[]{:S(2)}, u32[]{:S(2)}) collective-permute-start(bf16[2,256]{1,0:T(2,128)(2,1)S(1)} %collective-permute-done.9), channel_id=1, source_target_pairs={{0,240},{16,0},{32,16},{48,32},{64,48},{80,64},{96,80},{112,96},{1... | collective-permute-start | bytes 3080 | tf_op jit(solution)/shard_map/ppermute | solution.py:70
  34.0 1.0 collective-permute-done.10
  35.0 0.0 collective-permute-start.12
  35.0 0.3 collective-permute-done.11
  35.3 2.9 %collective-permute-start.13 = (bf16[2,256]{1,0:T(2,128)(2,1)S(1)}, bf16[2,256]{1,0:T(2,128)(2,1)S(1)}, u32[]{:S(2)}, u32[]{:S(2)}) collective-permute-start(bf16[2,256]{1,0:T(2,128)(2,1)S(1)} %collective-permute-done.11), channel_id=1, source_target_pairs={{0,240},{16,0},{32,16},{48,32},{64,48},{80,64},{96,80},{112,96},{1... | collective-permute-start | bytes 3080 | tf_op jit(solution)/shard_map/ppermute | solution.py:70
  38.2 1.0 collective-permute-done.12
  39.2 0.0 collective-permute-start.14
  39.2 0.3 collective-permute-done.13
  39.5 3.9 %collective-permute-done.14 = bf16[2,256]{1,0:T(2,128)(2,1)S(1)} collective-permute-done((bf16[2,256]{1,0:T(2,128)(2,1)S(1)}, bf16[2,256]{1,0:T(2,128)(2,1)S(1)}, u32[]{:S(2)}, u32[]{:S(2)}) %collective-permute-start.14) | collective-permute-done | bytes 1056 | tf_op jit(solution)/shard_map/ppermute | solution.py:62
  43.4 0.2 convolution_convert_fusion.2
  43.6 0.1 reshape.42
  43.7 3.7 %fusion.4 = bf16[16,16,144,16]{2,1,3,0:T(8,128)(2,1)} fusion(bf16[144,16,16,16]{0,2,3,1:T(8,128)(2,1)} %fusion.7, bf16[16,16,16]{2,1,0:T(8,128)(2,1)S(1)} %reshape.42), kind=kOutput, calls=%fused_computation.6 | convolution fusion | flops 19464192 | bytes 2367488 | tf_op jit(solution)/shard_map/pojml,oijln->poimn/dot_general | solution.py:41
  47.5 3.6 %copy.18 = bf16[144,16,256]{2,0,1:T(8,128)(2,1)} copy(bf16[144,16,256]{0,2,1:T(8,128)(2,1)} %bitcast.44) | data formatting | bytes 2359296 | tf_op jit(solution)/shard_map/convert_element_type | solution.py:42
  51.1 0.0 all-gather.2.cloned.1.call-update
  51.1 0.0 reduce-scatter.4.cloned.1.call-start
  51.2 110.0 %all-gather.2.cloned.1.call-done = bf16[2304,16,256]{2,0,1:T(8,128)(2,1)} async-done(((bf16[144,16,256]{2,0,1:T(8,128)(2,1)}), bf16[2304,16,256]{2,0,1:T(8,128)(2,1)}) %all-gather.2.cloned.1.call-update) | async-done | bytes 18874384 | tf_op jit(solution)/shard_map/all_gather | solution.py:76
  161.2 9.5 %convolution_bitcast_fusion = f32[144,2304]{1,0:T(8,128)S(1)} fusion(bf16[2304,16,256]{2,0,1:T(8,128)(2,1)} %all-gather.2.cloned.1.call-done, bf16[144,16,256]{0,2,1:T(8,128)(2,1)S(1)} %copy.14), kind=kOutput, calls=%fused_computation.1 | convolution fusion | flops 2717908992 | bytes 21381120 | tf_op jit(solution)/shard_map/dot_general | solution.py:78
  170.7 1.9 copy.25
  172.6 0.0 reduce-scatter.4.cloned.1.call-update
  172.6 80.7 %reduce-scatter.4.cloned.1.call-done = f32[144,144]{1,0:T(8,128)} async-done(((f32[2304,144]{1,0:T(8,128)}), f32[144,144]{1,0:T(8,128)}) %reduce-scatter.4.cloned.1.call-update) | async-done | bytes 82960
  253.3 1.7 copy.26
  (24 shorter events, 0.2 us)
Async XLA Ops:
  6.5 1.8 copy-start
  6.5 4.5 %copy-start.1 = (bf16[144,16,256]{2,1,0:T(8,128)(2,1)S(1)}, bf16[144,16,256]{2,1,0:T(8,128)(2,1)}, u32[]{:S(2)}) copy-start(bf16[144,16,256]{2,1,0:T(8,128)(2,1)} %param.6) | copy-start | bytes 3538948
  6.5 154.6 %all-gather.2.cloned.1.call-start = ((), (), s32[]{:S(2)}) async-start(), calls=%async_computation.1 | async-start | bytes 20054016 | tf_op jit(solution)/shard_map/all_gather | solution.py:76
  6.5 10.2 %collective-permute-start = (bf16[2,256]{1,0:T(2,128)(2,1)}, bf16[2,256]{1,0:T(2,128)(2,1)S(1)}, u32[]{:S(2)}, u32[]{:S(2)}) collective-permute-start(bf16[2,256]{1,0:T(2,128)(2,1)} %bitcast.46), channel_id=1, source_target_pairs={{0,16},{16,32},{32,48},{48,64},{64,80},{80,96},{96,112},{112,128},... | collective-permute-start | bytes 3080 | tf_op jit(solution)/shard_map/ppermute | solution.py:62
  6.6 10.5 %collective-permute-start.1 = (bf16[2,256]{1,0:T(2,128)(2,1)}, bf16[2,256]{1,0:T(2,128)(2,1)S(1)}, u32[]{:S(2)}, u32[]{:S(2)}) collective-permute-start(bf16[2,256]{1,0:T(2,128)(2,1)} %bitcast.47), channel_id=1, source_target_pairs={{0,240},{16,0},{32,16},{48,32},{64,48},{80,64},{96,80},{112,96},{1... | collective-permute-start | bytes 3080 | tf_op jit(solution)/shard_map/ppermute | solution.py:70
  9.4 2.9 %copy-start.2 = (bf16[1,2,256]{2,1,0:T(2,128)(2,1)S(1)}, bf16[1,2,256]{2,1,0:T(2,128)(2,1)}, u32[]{:S(2)}) copy-start(bf16[1,2,256]{2,1,0:T(2,128)(2,1)} %param.11) | copy-start | bytes 3076
  12.3 31.1 %copy-start.3 = (s32[1,16,1]{1,2,0:T(1,128)S(1)}, s32[1,16,1]{1,2,0:T(1,128)}, u32[]{:S(2)}) copy-start(s32[1,16,1]{1,2,0:T(1,128)} %param.10) | copy-start | bytes 196
  16.7 3.0 %collective-permute-start.2 = (bf16[2,256]{1,0:T(2,128)(2,1)S(1)}, bf16[2,256]{1,0:T(2,128)(2,1)S(1)}, u32[]{:S(2)}, u32[]{:S(2)}) collective-permute-start(bf16[2,256]{1,0:T(2,128)(2,1)S(1)} %collective-permute-done), channel_id=1, source_target_pairs={{0,16},{16,32},{32,48},{48,64},{64,80},{80,96},{96,112},{112,128},... | collective-permute-start | bytes 3080 | tf_op jit(solution)/shard_map/ppermute | solution.py:62
  17.0 2.8 %collective-permute-start.3 = (bf16[2,256]{1,0:T(2,128)(2,1)S(1)}, bf16[2,256]{1,0:T(2,128)(2,1)S(1)}, u32[]{:S(2)}, u32[]{:S(2)}) collective-permute-start(bf16[2,256]{1,0:T(2,128)(2,1)S(1)} %collective-permute-done.1), channel_id=1, source_target_pairs={{0,240},{16,0},{32,16},{48,32},{64,48},{80,64},{96,80},{112,96},{1... | collective-permute-start | bytes 3080 | tf_op jit(solution)/shard_map/ppermute | solution.py:70
  19.7 3.0 %collective-permute-start.4 = (bf16[2,256]{1,0:T(2,128)(2,1)S(1)}, bf16[2,256]{1,0:T(2,128)(2,1)S(1)}, u32[]{:S(2)}, u32[]{:S(2)}) collective-permute-start(bf16[2,256]{1,0:T(2,128)(2,1)S(1)} %collective-permute-done.2), channel_id=1, source_target_pairs={{0,16},{16,32},{32,48},{48,64},{64,80},{80,96},{96,112},{112,128},... | collective-permute-start | bytes 3080 | tf_op jit(solution)/shard_map/ppermute | solution.py:62
  19.8 3.0 %collective-permute-start.5 = (bf16[2,256]{1,0:T(2,128)(2,1)S(1)}, bf16[2,256]{1,0:T(2,128)(2,1)S(1)}, u32[]{:S(2)}, u32[]{:S(2)}) collective-permute-start(bf16[2,256]{1,0:T(2,128)(2,1)S(1)} %collective-permute-done.3), channel_id=1, source_target_pairs={{0,240},{16,0},{32,16},{48,32},{64,48},{80,64},{96,80},{112,96},{1... | collective-permute-start | bytes 3080 | tf_op jit(solution)/shard_map/ppermute | solution.py:70
  22.7 3.9 %collective-permute-start.6 = (bf16[2,256]{1,0:T(2,128)(2,1)S(1)}, bf16[2,256]{1,0:T(2,128)(2,1)S(1)}, u32[]{:S(2)}, u32[]{:S(2)}) collective-permute-start(bf16[2,256]{1,0:T(2,128)(2,1)S(1)} %collective-permute-done.4), channel_id=1, source_target_pairs={{0,16},{16,32},{32,48},{48,64},{64,80},{80,96},{96,112},{112,128},... | collective-permute-start | bytes 3080 | tf_op jit(solution)/shard_map/ppermute | solution.py:62
  22.8 4.1 %collective-permute-start.7 = (bf16[2,256]{1,0:T(2,128)(2,1)S(1)}, bf16[2,256]{1,0:T(2,128)(2,1)S(1)}, u32[]{:S(2)}, u32[]{:S(2)}) collective-permute-start(bf16[2,256]{1,0:T(2,128)(2,1)S(1)} %collective-permute-done.5), channel_id=1, source_target_pairs={{0,240},{16,0},{32,16},{48,32},{64,48},{80,64},{96,80},{112,96},{1... | collective-permute-start | bytes 3080 | tf_op jit(solution)/shard_map/ppermute | solution.py:70
  26.6 4.2 %collective-permute-start.8 = (bf16[2,256]{1,0:T(2,128)(2,1)S(1)}, bf16[2,256]{1,0:T(2,128)(2,1)S(1)}, u32[]{:S(2)}, u32[]{:S(2)}) collective-permute-start(bf16[2,256]{1,0:T(2,128)(2,1)S(1)} %collective-permute-done.6), channel_id=1, source_target_pairs={{0,16},{16,32},{32,48},{48,64},{64,80},{80,96},{96,112},{112,128},... | collective-permute-start | bytes 3080 | tf_op jit(solution)/shard_map/ppermute | solution.py:62
  26.9 4.2 %collective-permute-start.9 = (bf16[2,256]{1,0:T(2,128)(2,1)S(1)}, bf16[2,256]{1,0:T(2,128)(2,1)S(1)}, u32[]{:S(2)}, u32[]{:S(2)}) collective-permute-start(bf16[2,256]{1,0:T(2,128)(2,1)S(1)} %collective-permute-done.7), channel_id=1, source_target_pairs={{0,240},{16,0},{32,16},{48,32},{64,48},{80,64},{96,80},{112,96},{1... | collective-permute-start | bytes 3080 | tf_op jit(solution)/shard_map/ppermute | solution.py:70
  30.8 4.2 %collective-permute-start.10 = (bf16[2,256]{1,0:T(2,128)(2,1)S(1)}, bf16[2,256]{1,0:T(2,128)(2,1)S(1)}, u32[]{:S(2)}, u32[]{:S(2)}) collective-permute-start(bf16[2,256]{1,0:T(2,128)(2,1)S(1)} %collective-permute-done.8), channel_id=1, source_target_pairs={{0,16},{16,32},{32,48},{48,64},{64,80},{80,96},{96,112},{112,128},... | collective-permute-start | bytes 3080 | tf_op jit(solution)/shard_map/ppermute | solution.py:62
  31.1 4.2 %collective-permute-start.11 = (bf16[2,256]{1,0:T(2,128)(2,1)S(1)}, bf16[2,256]{1,0:T(2,128)(2,1)S(1)}, u32[]{:S(2)}, u32[]{:S(2)}) collective-permute-start(bf16[2,256]{1,0:T(2,128)(2,1)S(1)} %collective-permute-done.9), channel_id=1, source_target_pairs={{0,240},{16,0},{32,16},{48,32},{64,48},{80,64},{96,80},{112,96},{1... | collective-permute-start | bytes 3080 | tf_op jit(solution)/shard_map/ppermute | solution.py:70
  35.0 4.2 %collective-permute-start.12 = (bf16[2,256]{1,0:T(2,128)(2,1)S(1)}, bf16[2,256]{1,0:T(2,128)(2,1)S(1)}, u32[]{:S(2)}, u32[]{:S(2)}) collective-permute-start(bf16[2,256]{1,0:T(2,128)(2,1)S(1)} %collective-permute-done.10), channel_id=1, source_target_pairs={{0,16},{16,32},{32,48},{48,64},{64,80},{80,96},{96,112},{112,128},... | collective-permute-start | bytes 3080 | tf_op jit(solution)/shard_map/ppermute | solution.py:62
  35.3 4.2 %collective-permute-start.13 = (bf16[2,256]{1,0:T(2,128)(2,1)S(1)}, bf16[2,256]{1,0:T(2,128)(2,1)S(1)}, u32[]{:S(2)}, u32[]{:S(2)}) collective-permute-start(bf16[2,256]{1,0:T(2,128)(2,1)S(1)} %collective-permute-done.11), channel_id=1, source_target_pairs={{0,240},{16,0},{32,16},{48,32},{64,48},{80,64},{96,80},{112,96},{1... | collective-permute-start | bytes 3080 | tf_op jit(solution)/shard_map/ppermute | solution.py:70
  39.2 4.2 %collective-permute-start.14 = (bf16[2,256]{1,0:T(2,128)(2,1)S(1)}, bf16[2,256]{1,0:T(2,128)(2,1)S(1)}, u32[]{:S(2)}, u32[]{:S(2)}) collective-permute-start(bf16[2,256]{1,0:T(2,128)(2,1)S(1)} %collective-permute-done.12), channel_id=1, source_target_pairs={{0,16},{16,32},{32,48},{48,64},{64,80},{80,96},{96,112},{112,128},... | collective-permute-start | bytes 3080 | tf_op jit(solution)/shard_map/ppermute | solution.py:62
  51.1 202.2 %reduce-scatter.4.cloned.1.call-start = ((), (), s32[]{:S(2)}) async-start(), calls=%async_computation.2 | async-start | bytes 2506752
Sparse Core Ops, SparseCore 0:
  51.3 109.8 all-gather.1
  172.7 80.5 reduce-scatter.3
